TPU v7x, 32 devices: a whole 2x2x4 slice. The times are simulated.
32 devices in a mesh: src: 8 (over z, y), tgt: 4 (over x, core).
Axes of the slice: x: 2, y: 2, z: 4, core: 2. Of those that a mesh axis runs over, the one named last changes fastest.
Arguments:
- edge_state: bfloat16 [65536, 512], P(('src', 'tgt')), may hold values from -6 to 6
- atom_state: bfloat16 [8192, 512], P('src'), may hold values from -6 to 6
- edge_src: int32 [65536], P(('src', 'tgt')), may hold values from 0 to 1023, as said below
- edge_tgt: int32 [65536], P(('src', 'tgt')), may hold values from 0 to 1023, as said below
- reverse: int32 [65536], P(('src', 'tgt')), may hold values from 0 to 2047, as said below
- w_in: bfloat16 [3, 512, 512], replicated, may hold values from -0.25 to 0.25
- w_out: bfloat16 [3, 512, 512], replicated, may hold values from -0.25 to 0.25
- edge_gain: float32 [3, 512], replicated, may hold values from 0.25 to 1.75
- atom_gain: float32 [512], replicated, may hold values from 0.25 to 1.75
- atom_up: bfloat16 [512, 512], replicated, may hold values from -0.25 to 0.25
- atom_down: bfloat16 [512, 512], replicated, may hold values from -0.25 to 0.25
Outputs:
- edge_out: bfloat16 [65536, 512], P(('src', 'tgt'))
Inputs may be any that keep to these rules, and one draw needn't show every extreme that they name: edge_src is a local atom index within the edge's source block of 1024 atoms. edge_tgt is a local atom index within the edge's target block; the reverse edge's edge_src equals it.
All inputs are finite; a program needn't handle non-finite values.
Results may differ from a plain program's by a relative error of at most 0.0075.
Values may be sent and summed in bfloat16 or wider, within the bound.
A program may use at most 64 MiB of HBM per device.

v0:
```python
import jax
import jax.numpy as jnp
from jax import lax
from jax.sharding import PartitionSpec as P


def rms_scaled(values, scales):
    return values * lax.rsqrt(jnp.mean(values * values, axis=-1, keepdims=True) + 1e-06) * scales


def atom_update(summed, atom_gain, atom_up, atom_down):
    atom_normed = rms_scaled(summed, atom_gain).astype(jnp.bfloat16)
    atom_hidden = jax.nn.silu(
        jnp.dot(atom_normed, atom_up, preferred_element_type=jnp.float32)
    ).astype(jnp.bfloat16)
    return jnp.dot(atom_hidden, atom_down, preferred_element_type=jnp.float32).astype(jnp.bfloat16)


def shards(
    edge_state,
    atom_state,
    edge_src,
    edge_tgt,
    reverse,
    w_in,
    w_out,
    edge_gain,
    atom_gain,
    atom_up,
    atom_down,
):
    count_src = lax.axis_size("src")
    count_tgt = lax.axis_size("tgt")
    groups = count_src // count_tgt
    edge_rows = edge_state.shape[0]
    features = edge_state.shape[1]
    atom_block = atom_state.shape[0]
    rows_sub = edge_rows // (groups * count_src)
    sources = jnp.take(atom_state, edge_src, axis=0)
    initial = (edge_state.astype(jnp.float32) + sources.astype(jnp.float32)).astype(jnp.bfloat16)
    framed = initial.reshape(count_src, groups, rows_sub, features)
    spread = lax.all_to_all(framed, "tgt", split_axis=0, concat_axis=1, tiled=True)
    mirrored = lax.all_to_all(
        lax.all_to_all(spread, "src", split_axis=1, concat_axis=1, tiled=True),
        "tgt",
        split_axis=1,
        concat_axis=0,
        tiled=True,
    ).reshape(edge_rows, features)
    partner_rows = jnp.take(mirrored, reverse, axis=0)
    stream = initial.astype(jnp.float32)
    for layer in range(w_in.shape[0]):
        normed = rms_scaled(stream, edge_gain[layer]).astype(jnp.bfloat16)
        hidden = jax.nn.silu(
            jnp.dot(normed, w_in[layer], preferred_element_type=jnp.float32)
        ).astype(jnp.bfloat16)
        stream = stream + jnp.dot(hidden, w_out[layer], preferred_element_type=jnp.float32)
    merged = stream + partner_rows.astype(jnp.float32)
    message = merged.astype(jnp.bfloat16)
    subtile = jnp.arange(edge_rows, dtype=jnp.int32) // rows_sub % groups
    target_rows = subtile * atom_block + edge_tgt
    column_rows = groups * atom_block
    slots = jnp.arange(column_rows, dtype=jnp.int32)
    one_hot = (slots[:, None] == target_rows[None, :]).astype(jnp.bfloat16)
    summed = lax.psum(jnp.dot(one_hot, message, preferred_element_type=jnp.float32), "src")
    updated = atom_update(summed, atom_gain, atom_up, atom_down)
    returned = jnp.take(updated, target_rows, axis=0)
    return (merged + returned.astype(jnp.float32)).astype(jnp.bfloat16)


def solution(mesh):
    in_specs = (
        P(("src", "tgt"), None),
        P("src", None),
        P(("src", "tgt")),
        P(("src", "tgt")),
        P(("src", "tgt")),
        P(),
        P(),
        P(),
        P(),
        P(),
        P(),
    )
    out_specs = P(("src", "tgt"), None)
    return jax.shard_map(shards, mesh=mesh, in_specs=in_specs, out_specs=out_specs, check_vma=False)
```

profile of v0, /device:TPU:29, one launch (start us, length us, event | category | flops | bytes accessed | tf_op | source)
XLA Modules:
  0.0 361.6 jit_solution(9478223658099596428)
XLA Ops:
  8.0 7.5 %gather_fusion = bf16[2048,512]{1,0:T(8,128)(2,1)S(1)} fusion(bf16[1024,512]{1,0:T(8,128)(2,1)S(1)} %copy-done, s32[2048]{0:T(1024)S(1)} %fusion.47), kind=kCustom, calls=%fused_computation.2 | custom fusion | bytes 4202496 | tf_op jit(solution)/shard_map/jit(_take)/gather | solution.py:39
  15.6 2.4 copy.35
  18.0 4.0 %copy.34 = bf16[2048,512]{0,1:T(8,128)(2,1)} copy(bf16[2048,512]{1,0:T(8,128)(2,1)} %param.13) | data formatting | bytes 4194304 | tf_op args[0]
  21.9 3.2 fusion.2
  25.1 2.5 copy.46
  27.6 28.9 %all_to_all.38 = bf16[8,2,128,512]{3,2,1,0:T(8,128)(2,1)S(1)} all-to-all(bf16[8,2,128,512]{3,2,1,0:T(8,128)(2,1)} %bitcast.47), channel_id=1, replica_groups=mesh['src'=8,'tgt'=4] {'tgt'}, dimensions={0} | all-to-all | bytes 4194304 | tf_op jit(solution)/shard_map/all_to_all | solution.py:42
  58.3 5.4 %all-to-all-start.1 = ((bf16[2,8,128,512]{3,2,0,1:T(8,128)(2,1)}), bf16[2,8,128,512]{3,2,0,1:T(8,128)(2,1)}, u32[]{:S(2)}, u32[]{:S(2)}) async-start(bf16[2,8,128,512]{3,2,0,1:T(8,128)(2,1)} %copy.39), calls=%async_computation.1 | async-start | bytes 4194304 | tf_op jit(solution)/shard_map/all_to_all | solution.py:44
  63.7 6.4 %multiply_reduce_fusion.2 = (f32[2048]{0:T(1024)S(1)}, f32[2048,512]{0,1:T(8,128)}) fusion(bf16[3,512,512]{2,1,0:T(8,128)(2,1)} %param.19, bf16[2048,512]{0,1:T(8,128)(2,1)S(1)} %get-tuple-element.9, f32[512]{0:T(512)S(1)} %bitcast.50, f32[2048]{0:T(1024)S(1)} %add_rsqrt_fusion.3, bf16[3,512,512]{2,1,0:T(8,128)(2,1)} %param.18), kind=kOutput, calls=%fused_computation.22 | convolution fusion | flops 2161113088 | bytes 9455616 | tf_op jit(solution)/shard_map/dot_general | solution.py:57
  70.1 40.3 %all-to-all-done.1 = bf16[2,8,128,512]{3,2,0,1:T(8,128)(2,1)} async-done(((bf16[2,8,128,512]{3,2,0,1:T(8,128)(2,1)}), bf16[2,8,128,512]{3,2,0,1:T(8,128)(2,1)}, u32[]{:S(2)}, u32[]{:S(2)}) %all-to-all-start.1) | async-done | bytes 2097184 | tf_op jit(solution)/shard_map/all_to_all | solution.py:44
  110.4 4.1 %all-to-all-start.2 = ((bf16[2,8,128,512]{3,2,0,1:T(8,128)(2,1)}), bf16[2,8,128,512]{3,2,0,1:T(8,128)(2,1)S(1)}, u32[]{:S(2)}, u32[]{:S(2)}) async-start(bf16[2,8,128,512]{3,2,0,1:T(8,128)(2,1)} %all-to-all-done.1), calls=%async_computation.2 | async-start | bytes 4194304 | tf_op jit(solution)/shard_map/all_to_all | solution.py:43
  114.5 8.9 %multiply_reduce_fusion.1 = (f32[2048]{0:T(1024)S(1)}, f32[2048,512]{0,1:T(8,128)}) fusion(f32[2048,512]{0,1:T(8,128)} %get-tuple-element.14, bf16[3,512,512]{2,1,0:T(8,128)(2,1)} %param.19, f32[512]{0:T(512)S(1)} %bitcast.49, f32[2048]{0:T(1024)S(1)} %add_rsqrt_fusion.2, bf16[3,512,512]{2,1,0:T(8,128)(2,1)} %param.18), kind=kOutput, calls=%fused_computation.19 | convolution fusion | flops 2159015936 | bytes 13649920 | tf_op jit(solution)/shard_map/dot_general | solution.py:57
  123.4 15.8 %all-to-all-done.2 = bf16[2,8,128,512]{3,2,0,1:T(8,128)(2,1)S(1)} async-done(((bf16[2,8,128,512]{3,2,0,1:T(8,128)(2,1)}), bf16[2,8,128,512]{3,2,0,1:T(8,128)(2,1)S(1)}, u32[]{:S(2)}, u32[]{:S(2)}) %all-to-all-start.2) | async-done | bytes 2097184 | tf_op jit(solution)/shard_map/all_to_all | solution.py:43
  140.5 1.8 copy.41
  142.3 9.4 %gather_fusion.1 = bf16[2048,512]{1,0:T(8,128)(2,1)} fusion(bf16[2048,512]{1,0:T(8,128)(2,1)S(1)} %bitcast.43, s32[2048]{0:T(1024)S(1)} %fusion.48), kind=kCustom, calls=%fused_computation.clone | custom fusion | bytes 4202496 | tf_op jit(solution)/shard_map/jit(_take)/gather | solution.py:50
  151.7 2.9 copy.42
  154.6 8.9 %convert_add_fusion.1 = f32[2048,512]{0,1:T(8,128)} fusion(f32[2048,512]{0,1:T(8,128)} %get-tuple-element.16, bf16[2048,512]{0,1:T(8,128)(2,1)S(1)} %copy.42, pred[2048]{0:T(1024)(128)(4,1)S(1)} %compare_and_fusion.1, f32[512]{0:T(512)S(1)} %bitcast.48, f32[2048]{0:T(1024)S(1)} %add_rsqrt_fusion.1, bf16[3,512,512]{2,1,0:T(8,128)(2,1)} %param.19, ...), kind=kOutput, calls=%fused_computation.16 | convolution fusion | flops 2160066560 | bytes 15740928 | tf_op jit(solution)/shard_map/dot_general | solution.py:57
  163.5 8.2 %fusion = f32[2048,512]{1,0:T(8,128)} fusion(s32[2048]{0:T(1024)S(1)} %get-tuple-element.7, f32[2048,512]{0,1:T(8,128)} %convert_add_fusion.1), kind=kOutput, calls=%fused_computation.4 | convolution fusion | flops 4300210176 | bytes 8396800 | tf_op jit(solution)/shard_map/dot_general | solution.py:65
  171.8 154.8 %all-reduce.2.cloned.1.call-done = f32[2048,512]{1,0:T(8,128)} async-done(((f32[2048,512]{1,0:T(8,128)}), f32[2048,512]{1,0:T(8,128)}) %all-reduce.2.cloned.1.call-update) | async-done | bytes 4194320 | tf_op jit(solution)/shard_map/psum | solution.py:65
  326.6 2.5 multiply_reduce_fusion
  329.2 5.3 %convolution_convert_fusion = bf16[2048,512]{1,0:T(8,128)(2,1)S(1)} fusion(bf16[512,512]{1,0:T(8,128)(2,1)} %param.23, bf16[512,512]{1,0:T(8,128)(2,1)} %param.22, f32[2048,512]{1,0:T(8,128)} %all-reduce.2.cloned.1.call-done, f32[512]{0:T(512)S(1)} %copy-done.5, f32[2048]{0:T(1024)S(1)} %add_rsqrt_fusion), kind=kOutput, calls=%fused_computation.26 | convolution fusion | flops 2156920832 | bytes 7350272 | tf_op jit(solution)/shard_map/dot_general | solution.py:16
  334.5 9.2 %gather_fusion.2 = bf16[2048,512]{1,0:T(8,128)(2,1)} fusion(bf16[2048,512]{1,0:T(8,128)(2,1)S(1)} %convolution_convert_fusion, s32[2048]{0:T(1024)S(1)} %fusion.49), kind=kCustom, calls=%fused_computation.1.clone | custom fusion | bytes 4202496 | tf_op jit(solution)/shard_map/jit(_take)/gather | solution.py:67
  343.7 2.9 copy.43
  346.6 4.2 %add_convert_fusion = bf16[2048,512]{0,1:T(8,128)(2,1)} fusion(f32[2048,512]{0,1:T(8,128)} %convert_add_fusion.1, bf16[2048,512]{0,1:T(8,128)(2,1)S(1)} %copy.43, pred[2048]{0:T(1024)(128)(4,1)S(1)} %get-tuple-element.6), kind=kLoop, calls=%fused_computation.12 | loop fusion | flops 4194304 | bytes 8390656 | tf_op jit(solution)/shard_map/convert_element_type | solution.py:68
  350.8 3.9 %copy.44 = bf16[2048,512]{1,0:T(8,128)(2,1)} copy(bf16[2048,512]{0,1:T(8,128)(2,1)} %add_convert_fusion) | data formatting | bytes 4194304 | tf_op jit(solution)/shard_map/convert_element_type | solution.py:68
  (27 shorter events, 4.6 us)
Async XLA Ops:
  6.5 1.5 copy-start
  56.7 7.0 %copy-start.4 = (f32[3,512]{1,0:T(4,128)S(1)}, f32[3,512]{1,0:T(4,128)}, u32[]{:S(2)}) copy-start(f32[3,512]{1,0:T(4,128)} %param.20) | copy-start | bytes 18436
  56.7 7.0 %copy-start.2 = (s32[2048]{0:T(1024)S(1)}, s32[2048]{0:T(1024)}, u32[]{:S(2)}) copy-start(s32[2048]{0:T(1024)} %param.17) | copy-start | bytes 24580
  58.3 52.2 %all-to-all-start.1 = ((bf16[2,8,128,512]{3,2,0,1:T(8,128)(2,1)}), bf16[2,8,128,512]{3,2,0,1:T(8,128)(2,1)}, u32[]{:S(2)}, u32[]{:S(2)}) async-start(bf16[2,8,128,512]{3,2,0,1:T(8,128)(2,1)} %copy.39), calls=%async_computation.1 | async-start | bytes 4194304 | tf_op jit(solution)/shard_map/all_to_all | solution.py:44
  110.4 28.8 %all-to-all-start.2 = ((bf16[2,8,128,512]{3,2,0,1:T(8,128)(2,1)}), bf16[2,8,128,512]{3,2,0,1:T(8,128)(2,1)S(1)}, u32[]{:S(2)}, u32[]{:S(2)}) async-start(bf16[2,8,128,512]{3,2,0,1:T(8,128)(2,1)} %all-to-all-done.1), calls=%async_computation.2 | async-start | bytes 4194304 | tf_op jit(solution)/shard_map/all_to_all | solution.py:43
  114.5 212.1 %all-reduce.2.cloned.1.call-start = ((), (), s32[]{:S(2)}) async-start(), calls=%async_computation.3 | async-start | bytes 8388608 | tf_op jit(solution)/shard_map/psum | solution.py:65
  114.5 8.9 %copy-start.3 = (s32[2048]{0:T(1024)S(1)}, s32[2048]{0:T(1024)}, u32[]{:S(2)}) copy-start(s32[2048]{0:T(1024)} %param.16) | copy-start | bytes 24580
  139.2 1.3 copy-start.1
  171.8 157.4 %copy-start.5 = (f32[512]{0:T(512)S(1)}, f32[512]{0:T(512)}, u32[]{:S(2)}) copy-start(f32[512]{0:T(512)} %param.21) | copy-start | bytes 6148
Sparse Core Ops, SparseCore 0:
  171.9 154.6 all-reduce.1
where the time goes:
time: 366 us; the launch traced here: 362 us
  waiting for transfers between devices  211 us (58%)
  local copies, waits for them, and re-layouts  49.6 us (14%)
  matrix products  37.7 us (10%)
  blocking collectives  28.9 us (8%)
  between operations  13.5 us (4%)
  other arithmetic  11.5 us (3%)
  starting transfers between devices  9.51 us (3%)
    psum x1, waiting for transfers between devices, shards(): lax.psum(jnp.dot(one_hot, message, preferred_element_type=jnp.float32), '...  155 us
    all_to_all x1, waiting for transfers between devices, shards(): lax.all_to_all(spread, 'src', split_axis=1, concat_axis=1, tiled=True)  40.3 us
    all_to_all x1, blocking collectives, shards(): lax.all_to_all(framed, 'tgt', split_axis=0, concat_axis=1, tiled=True)  28.9 us
    dot_general x3, matrix products, shards(): jnp.dot(hidden, w_out[layer], preferred_element_type=jnp.float32)  24.1 us
    all_to_all x1, waiting for transfers between devices, shards(): lax.all_to_all(lax.all_to_all(spread, 'src', split_axis=1, concat_axis=1,...  15.8 us
    gather x2, local copies, waits for them, and re-layouts, shards(): partner_rows = jnp.take(mirrored, reverse, axis=0)  12.3 us
    gather x2, local copies, waits for them, and re-layouts, shards(): returned = jnp.take(updated, target_rows, axis=0)  12.1 us
    gather x2, local copies, waits for them, and re-layouts, shards(): sources = jnp.take(atom_state, edge_src, axis=0)  9.91 us
  transfers between devices with their start and end apart: 3, of which 3 were waited for; matrix products, arithmetic and copies ran while one was open for 4% of the time, Pallas kernels for 0%

commit v1 on v0

v1 whole, which is shorter than its diff:
```python
import functools

import jax
import jax.numpy as jnp
from jax import lax
from jax.experimental import pallas as pl
from jax.experimental.pallas import tpu as pltpu
from jax.sharding import PartitionSpec as P

F32 = jnp.float32
BF16 = jnp.bfloat16


def rms_scaled(values, scales):
    return values * lax.rsqrt(jnp.mean(values * values, axis=-1, keepdims=True) + 1e-06) * scales


def picks(column, width):
    slots = lax.broadcasted_iota(jnp.int32, (column.shape[0], width), 1)
    return jnp.where(slots == column, 1.0, 0.0).astype(BF16)


def start_kernel(order, edge_ref, cols_ref, atom_ref, start_ref):
    rows, width = start_ref.shape
    sources = jnp.dot(picks(cols_ref[0, :, 0:1], atom_ref.shape[0]), atom_ref[...], preferred_element_type=F32)
    edges = edge_ref[...].reshape(rows, width).astype(F32)
    start_ref[...] = (edges + sources).astype(BF16)


def stream_kernel(start_ref, w_in_ref, w_out_ref, gain_ref, u_ref):
    stream = start_ref[...].astype(F32)
    for layer in range(w_in_ref.shape[0]):
        normed = rms_scaled(stream, gain_ref[layer : layer + 1]).astype(BF16)
        hidden = jax.nn.silu(jnp.dot(normed, w_in_ref[layer], preferred_element_type=F32)).astype(BF16)
        stream = stream + jnp.dot(hidden, w_out_ref[layer], preferred_element_type=F32)
    u_ref[...] = stream


def merge_kernel(groups, order, *refs):
    u_refs, recv_refs = refs[:groups], refs[groups : 2 * groups]
    cols_ref, tgt_ref, merged_ref, part_ref, total = refs[2 * groups :]
    turn, tile = pl.program_id(0), pl.program_id(1)

    @pl.when(tile == 0)
    def _():
        total[...] = jnp.zeros_like(total)

    for s in range(groups):

        @pl.when(turn == s)
        def _():
            partner = jnp.dot(
                picks(cols_ref[0, :, 1:2], recv_refs[s].shape[0]), recv_refs[s][...], preferred_element_type=F32
            )
            merged = u_refs[s][...] + partner
            merged_ref[0] = merged
            slots = lax.broadcasted_iota(jnp.int32, (total.shape[0], merged.shape[0]), 0)
            chosen = jnp.where(slots == tgt_ref[0], 1.0, 0.0).astype(BF16)
            total[...] += jnp.dot(chosen, merged.astype(BF16), preferred_element_type=F32)

    @pl.when(tile == pl.num_programs(1) - 1)
    def _():
        part_ref[0] = total[...].astype(part_ref.dtype)


def atom_kernel(sum_ref, gain_ref, up_ref, down_ref, new_ref):
    normed = rms_scaled(sum_ref[...].astype(F32), gain_ref[...]).astype(BF16)
    hidden = jax.nn.silu(jnp.dot(normed, up_ref[...], preferred_element_type=F32)).astype(BF16)
    new_ref[...] = jnp.dot(hidden, down_ref[...], preferred_element_type=F32).astype(BF16)


def finish_kernel(order, merged_ref, cols_ref, new_ref, out_ref):
    returned = jnp.dot(picks(cols_ref[0, :, 2:3], new_ref.shape[0]), new_ref[...], preferred_element_type=F32)
    out_ref[...] = (merged_ref[0] + returned).astype(BF16).reshape(out_ref.shape)


def shards(
    edge_state,
    atom_state,
    edge_src,
    edge_tgt,
    reverse,
    w_in,
    w_out,
    edge_gain,
    atom_gain,
    atom_up,
    atom_down,
):
    count_src = lax.axis_size("src")
    count_tgt = lax.axis_size("tgt")
    groups = count_src // count_tgt
    edge_rows, width = edge_state.shape
    atoms = atom_state.shape[0]
    rows_sub = edge_rows // (groups * count_src)
    rows = count_src * rows_sub
    slices = max(1, 256 // rows_sub)
    tile = slices * rows_sub
    tiles = rows // tile
    row = lax.axis_index("src")
    order = jnp.stack([lax.rem(s - row % groups + groups, groups) for s in range(groups)]).astype(jnp.int32)

    def by_group(index):
        return index.reshape(count_src, groups, rows_sub).transpose(1, 0, 2).reshape(groups, rows)

    spot = reverse // (groups * rows_sub) * rows_sub + reverse % rows_sub
    targets = by_group(edge_tgt)
    columns = jnp.stack([by_group(edge_src), by_group(spot), targets, targets], axis=-1)
    lines = targets.reshape(groups, 1, rows)
    framed = edge_state.reshape(count_src, groups, rows_sub, width)
    layers = w_in.shape[0]
    whole = pl.BlockSpec(memory_space=pltpu.VMEM)

    starts, received, streams = [], [], []
    for s in range(groups):
        start = pl.pallas_call(
            start_kernel,
            name=f"start{s}",
            grid_spec=pltpu.PrefetchScalarGridSpec(
                num_scalar_prefetch=1,
                grid=(tiles,),
                in_specs=[
                    pl.BlockSpec((slices, None, rows_sub, width), lambda t, order, s=s: (t, order[s], 0, 0)),
                    pl.BlockSpec((1, tile, 4), lambda t, order, s=s: (order[s], t, 0)),
                    pl.BlockSpec((atoms, width), lambda t, order: (0, 0)),
                ],
                out_specs=pl.BlockSpec((tile, width), lambda t, order: (t, 0)),
            ),
            out_shape=jax.ShapeDtypeStruct((rows, width), BF16),
        )(order, framed, columns, atom_state)
        pairs = []
        for i in range(count_src):
            for j in range(count_tgt):
                to = (j * groups + (s - i) % groups) * count_tgt + i // groups
                pairs.append((i * count_tgt + j, to))
        starts.append(start)
        received.append(lax.ppermute(start, ("src", "tgt"), pairs))
    wide = min(rows, 512)
    for s in range(groups):
        streams.append(
            pl.pallas_call(
                stream_kernel,
                name=f"stream{s}",
                grid=(rows // wide,),
                in_specs=[
                    pl.BlockSpec((wide, width), lambda t: (t, 0)),
                    pl.BlockSpec(w_in.shape, lambda t: (0, 0, 0)),
                    pl.BlockSpec(w_out.shape, lambda t: (0, 0, 0)),
                    pl.BlockSpec(edge_gain.shape, lambda t: (0, 0)),
                ],
                out_specs=pl.BlockSpec((wide, width), lambda t: (t, 0)),
                out_shape=jax.ShapeDtypeStruct((rows, width), F32),
                cost_estimate=pl.CostEstimate(
                    flops=4 * layers * rows * width * width,
                    bytes_accessed=6 * rows * width + 4 * layers * width * width,
                    transcendentals=layers * rows * width,
                ),
            )(starts[s], w_in, w_out, edge_gain)
        )
    merged, part = pl.pallas_call(
        functools.partial(merge_kernel, groups),
        name="merge",
        grid_spec=pltpu.PrefetchScalarGridSpec(
            num_scalar_prefetch=1,
            grid=(groups, tiles),
            in_specs=[
                pl.BlockSpec((tile, width), lambda g, t, order, s=s: (jnp.where(g == s, t, jnp.where(g < s, 0, tiles - 1)), 0))
                for s in range(groups)
            ]
            + [pl.BlockSpec((rows, width), lambda g, t, order: (0, 0)) for s in range(groups)]
            + [
                pl.BlockSpec((1, tile, 4), lambda g, t, order: (order[g], t, 0)),
                pl.BlockSpec((1, 1, tile), lambda g, t, order: (order[g], 0, t)),
            ],
            out_specs=[
                pl.BlockSpec((1, tile, width), lambda g, t, order: (g, t, 0)),
                pl.BlockSpec((1, atoms, width), lambda g, t, order: (order[g], 0, 0)),
            ],
            scratch_shapes=[pltpu.VMEM((atoms, width), F32)],
        ),
        out_shape=[
            jax.ShapeDtypeStruct((groups, rows, width), F32),
            jax.ShapeDtypeStruct((groups, atoms, width), BF16),
        ],
    )(order, *streams, *received, columns, lines)
    summed = lax.psum_scatter(part.reshape(groups * atoms, width), "src", scatter_dimension=0, tiled=True)
    updated = pl.pallas_call(
        atom_kernel,
        name="atoms",
        in_specs=[whole] * 4,
        out_specs=whole,
        out_shape=jax.ShapeDtypeStruct(summed.shape, BF16),
    )(summed, atom_gain.reshape(1, width), atom_up, atom_down)
    returned = lax.all_gather(updated, "src", axis=0, tiled=True)
    out = pl.pallas_call(
        finish_kernel,
        name="finish",
        grid_spec=pltpu.PrefetchScalarGridSpec(
            num_scalar_prefetch=1,
            grid=(groups, tiles),
            in_specs=[
                pl.BlockSpec((1, tile, width), lambda g, t, order: (g, t, 0)),
                pl.BlockSpec((1, tile, 4), lambda g, t, order: (order[g], t, 0)),
                pl.BlockSpec((atoms, width), lambda g, t, order: (order[g], 0)),
            ],
            out_specs=pl.BlockSpec((slices, None, rows_sub, width), lambda g, t, order: (t, order[g], 0, 0)),
        ),
        out_shape=jax.ShapeDtypeStruct(framed.shape, BF16),
    )(order, merged, columns, returned)
    return out.reshape(edge_rows, width)


def solution(mesh):
    in_specs = (
        P(("src", "tgt"), None),
        P("src", None),
        P(("src", "tgt")),
        P(("src", "tgt")),
        P(("src", "tgt")),
        P(),
        P(),
        P(),
        P(),
        P(),
        P(),
    )
    out_specs = P(("src", "tgt"), None)
    return jax.shard_map(shards, mesh=mesh, in_specs=in_specs, out_specs=out_specs, check_vma=False)
```

time: 366 us -> 265 us (0.72)
  the two profiles are of different devices: /device:TPU:29 before, /device:TPU:0 now
where the time goes in v1:
time: 265 us; the launch traced here: 264 us
  waiting for transfers between devices  188 us (71%)
  Pallas kernels  51.1 us (19%)
  between operations  13.5 us (5%)
  starting transfers between devices  4.91 us (2%)
  local copies, waits for them, and re-layouts  3.67 us (1%)
  other arithmetic  3.3 us (1%)
    reduce_scatter x1, waiting for transfers between devices, shards(): lax.psum_scatter(part.reshape(groups * atoms, width), 'src', scatter_dime...  140 us
    all_gather x1, waiting for transfers between devices, shards(): returned = lax.all_gather(updated, 'src', axis=0, tiled=True)  48.3 us
    pallas_call x2, Pallas kernels, shards(): pl.pallas_call(stream_kernel, name=f'stream{s}', grid=(rows // wide,), in...  14.6 us
    pallas_call x1, Pallas kernels, shards(): pl.pallas_call(functools.partial(merge_kernel, groups), name='merge', gri...  13.1 us
    pallas_call x2, Pallas kernels, shards(): pl.pallas_call(start_kernel, name=f'start{s}', grid_spec=pltpu.PrefetchSc...  11.2 us
    pallas_call x1, Pallas kernels, shards(): pl.pallas_call(finish_kernel, name='finish', grid_spec=pltpu.PrefetchScal...  9.59 us
  transfers between devices with their start and end apart: 4, of which 2 were waited for; matrix products, arithmetic and copies ran while one was open for 0% of the time, Pallas kernels for 8%

profile of v1, /device:TPU:0, one launch (start us, length us, event | category | flops | bytes accessed | tf_op | source)
XLA Modules:
  0.0 264.3 jit_solution(16755419750128558962)
XLA Ops:
  6.5 0.7 fusion.2
  7.3 0.4 copy.27
  7.6 1.1 copy.26
  8.7 0.4 copy.28
  9.1 0.6 pad_add_fusion.1.order
  9.7 1.9 pad_add_fusion.cols_ref.refs_4_
  11.7 5.6 %start0.1.start_ref = bf16[1024,512]{1,0:T(8,128)(2,1)} custom-call(s32[2]{0:T(128)} %pad_add_fusion.1.order, bf16[8,2,128,512]{3,2,1,0:T(8,128)(2,1)} %bitcast.22, s32[2,1024,4]{2,1,0:T(8,128)} %pad_add_fusion.cols_ref.refs_4_, bf16[1024,512]{1,0:T(8,128)(2,1)} %atom_ref.3), custom_call_target="tpu_custom_call" | custom-call | tf_op jit(solution)/shard_map/start0/pallas_call | solution.py:116
  17.3 1.9 collective-permute-start
  19.1 5.6 %start1.1.start_ref = bf16[1024,512]{1,0:T(8,128)(2,1)} custom-call(s32[2]{0:T(128)} %pad_add_fusion.1.order, bf16[8,2,128,512]{3,2,1,0:T(8,128)(2,1)} %bitcast.23, s32[2,1024,4]{2,1,0:T(8,128)} %pad_add_fusion.cols_ref.refs_4_, bf16[1024,512]{1,0:T(8,128)(2,1)} %atom_ref.3), custom_call_target="tpu_custom_call" | custom-call | tf_op jit(solution)/shard_map/start1/pallas_call | solution.py:116
  24.7 3.0 %collective-permute-start.1 = (bf16[1024,512]{1,0:T(8,128)(2,1)}, bf16[1024,512]{1,0:T(8,128)(2,1)S(1)}, u32[]{:S(2)}, u32[]{:S(2)}) collective-permute-start(bf16[1024,512]{1,0:T(8,128)(2,1)} %start1.1.start_ref), channel_id=1, source_target_pairs={{0,4},{1,12},{2,20},{3,28},{4,0},{5,8},{6,16},{7,24},{8,5},{9,13},... | collective-permute-start | bytes 3145736 | tf_op jit(solution)/shard_map/ppermute | solution.py:137
  27.7 0.6 copy.30
  28.3 7.3 %stream0.1.refs_0_ = f32[1024,512]{1,0:T(8,128)} custom-call(bf16[1024,512]{1,0:T(8,128)(2,1)} %start0.1.start_ref, bf16[3,512,512]{2,1,0:T(8,128)(2,1)} %w_in_ref.3, bf16[3,512,512]{2,1,0:T(8,128)(2,1)} %w_out_ref.3, f32[3,512]{1,0:T(4,128)} %gain_ref.3), custom_call_target="tpu_custom_call" | custom-call | flops 3221225472 | bytes 6291456 | tf_op jit(solution)/shard_map/stream0/pallas_call | solution.py:141
  35.6 7.3 %stream1.1.refs_1_ = f32[1024,512]{1,0:T(8,128)} custom-call(bf16[1024,512]{1,0:T(8,128)(2,1)} %start1.1.start_ref, bf16[3,512,512]{2,1,0:T(8,128)(2,1)} %w_in_ref.3, bf16[3,512,512]{2,1,0:T(8,128)(2,1)} %w_out_ref.3, f32[3,512]{1,0:T(4,128)} %gain_ref.3), custom_call_target="tpu_custom_call" | custom-call | flops 3221225472 | bytes 6291456 | tf_op jit(solution)/shard_map/stream1/pallas_call | solution.py:141
  42.9 0.0 collective-permute-done.refs_2_
  42.9 0.9 copy-done
  43.8 0.3 copy-done.1
  44.2 13.1 %merge.1 = (f32[2,1024,512]{2,1,0:T(8,128)}, bf16[2,1024,512]{2,1,0:T(8,128)(2,1)}) custom-call(s32[2]{0:T(128)} %pad_add_fusion.1.order, f32[1024,512]{1,0:T(8,128)} %stream0.1.refs_0_, f32[1024,512]{1,0:T(8,128)} %stream1.1.refs_1_, bf16[1024,512]{1,0:T(8,128)(2,1)} %copy-done, bf16[1024,512]{1,0:T(8,128)(2,1)} %copy-done.1, ...), custom_call_target="tpu_custom_call" | custom-call | tf_op jit(solution)/shard_map/merge/pallas_call | solution.py:160
  57.3 0.0 reduce-scatter.2.cloned.1.call-update
  57.3 0.0 all-gather.2.cloned.1.call-start
  57.4 139.6 %reduce-scatter.2.cloned.1.call-done.sum_ref = bf16[256,512]{1,0:T(8,128)(2,1)} async-done(((bf16[2048,512]{1,0:T(8,128)(2,1)}), bf16[256,512]{1,0:T(8,128)(2,1)}) %reduce-scatter.2.cloned.1.call-update) | async-done | bytes 262160 | tf_op jit(solution)/shard_map/reduce_scatter | solution.py:186
  197.0 2.6 atoms.1
  199.5 0.0 all-gather.2.cloned.1.call-update
  199.6 48.3 %all-gather.2.cloned.1.call-done.new_ref = bf16[2048,512]{1,0:T(8,128)(2,1)} async-done(((bf16[256,512]{1,0:T(8,128)(2,1)}), bf16[2048,512]{1,0:T(8,128)(2,1)}) %all-gather.2.cloned.1.call-update) | async-done | bytes 2097168 | tf_op jit(solution)/shard_map/all_gather | solution.py:194
  247.8 9.6 %finish.1 = bf16[8,2,128,512]{3,2,1,0:T(8,128)(2,1)} custom-call(s32[2]{0:T(128)} %pad_add_fusion.1.order, f32[2,1024,512]{2,1,0:T(8,128)} %get-tuple-element.7.merged_ref, s32[2,1024,4]{2,1,0:T(8,128)} %pad_add_fusion.cols_ref.refs_4_, bf16[2048,512]{1,0:T(8,128)(2,1)} %all-gather.2.cloned.1.call-done.new_ref), custom_call_target="tpu_custom_call" | custom-call | tf_op jit(solution)/shard_map/finish/pallas_call | solution.py:195
  (6 shorter events, 0.0 us)
Async XLA Ops:
  6.5 2.2 copy-start.2
  6.5 190.4 %reduce-scatter.2.cloned.1.call-start = ((), (), s32[]{:S(2)}) async-start(), calls=%async_computation.1 | async-start | bytes 2359296 | tf_op jit(solution)/shard_map/reduce_scatter | solution.py:186
  17.3 25.6 %collective-permute-start = (bf16[1024,512]{1,0:T(8,128)(2,1)}, bf16[1024,512]{1,0:T(8,128)(2,1)S(1)}, u32[]{:S(2)}, u32[]{:S(2)}) collective-permute-start(bf16[1024,512]{1,0:T(8,128)(2,1)} %start0.1.start_ref), channel_id=1, source_target_pairs={{0,0},{1,8},{2,16},{3,24},{4,4},{5,12},{6,20},{7,28},{8,1},{9,9},{... | collective-permute-start | bytes 3145736 | tf_op jit(solution)/shard_map/ppermute | solution.py:137
  24.7 18.2 %collective-permute-start.1 = (bf16[1024,512]{1,0:T(8,128)(2,1)}, bf16[1024,512]{1,0:T(8,128)(2,1)S(1)}, u32[]{:S(2)}, u32[]{:S(2)}) collective-permute-start(bf16[1024,512]{1,0:T(8,128)(2,1)} %start1.1.start_ref), channel_id=1, source_target_pairs={{0,4},{1,12},{2,20},{3,28},{4,0},{5,8},{6,16},{7,24},{8,5},{9,13},... | collective-permute-start | bytes 3145736 | tf_op jit(solution)/shard_map/ppermute | solution.py:137
  42.9 1.0 copy-start
  42.9 1.3 copy-start.1
  57.3 190.5 %all-gather.2.cloned.1.call-start = ((), (), s32[]{:S(2)}) async-start(), calls=%async_computation.2 | async-start | bytes 2359296 | tf_op jit(solution)/shard_map/all_gather | solution.py:194
Sparse Core Ops, SparseCore 0:
  57.5 139.4 reduce-scatter.1
  199.7 48.1 all-gather.1

commit v2 on v1

--- a/solution.py
+++ b/solution.py
@@ -63,10 +63,53 @@
         part_ref[0] = total[...].astype(part_ref.dtype)
 
 
-def atom_kernel(sum_ref, gain_ref, up_ref, down_ref, new_ref):
-    normed = rms_scaled(sum_ref[...].astype(F32), gain_ref[...]).astype(BF16)
+def exchange_kernel(count, part_ref, gain_ref, up_ref, down_ref, new_ref, inbox, sent, landed, sent_new, landed_new):
+    me = lax.axis_index("src")
+    piece = part_ref.shape[0] // count
+
+    def slot(owner):
+        return pl.ds(pl.multiple_of(owner * piece, piece), piece)
+
+    peers = [lax.rem(me + step, count) for step in range(1, count)]
+    barrier = pltpu.get_barrier_semaphore()
+    for peer in peers:
+        pl.semaphore_signal(barrier, inc=1, device_id={"src": peer}, device_id_type=pl.DeviceIdType.MESH)
+    pl.semaphore_wait(barrier, count - 1)
+    shares = []
+    for step, peer in enumerate(peers):
+        share = pltpu.make_async_remote_copy(
+            src_ref=part_ref.at[slot(peer)],
+            dst_ref=inbox.at[step],
+            send_sem=sent.at[step],
+            recv_sem=landed.at[step],
+            device_id={"src": peer},
+            device_id_type=pl.DeviceIdType.MESH,
+        )
+        share.start()
+        shares.append(share)
+    total = part_ref[slot(me)].astype(F32)
+    for step, share in enumerate(shares):
+        share.wait_recv()
+        total = total + inbox[step].astype(F32)
+    normed = rms_scaled(total, gain_ref[...]).astype(BF16)
     hidden = jax.nn.silu(jnp.dot(normed, up_ref[...], preferred_element_type=F32)).astype(BF16)
-    new_ref[...] = jnp.dot(hidden, down_ref[...], preferred_element_type=F32).astype(BF16)
+    new_ref[slot(me)] = jnp.dot(hidden, down_ref[...], preferred_element_type=F32).astype(BF16)
+    spreads = []
+    for step, peer in enumerate(peers):
+        spread = pltpu.make_async_remote_copy(
+            src_ref=new_ref.at[slot(me)],
+            dst_ref=new_ref.at[slot(me)],
+            send_sem=sent_new.at[step],
+            recv_sem=landed_new.at[step],
+            device_id={"src": peer},
+            device_id_type=pl.DeviceIdType.MESH,
+        )
+        spread.start()
+        spreads.append(spread)
+    for share in shares:
+        share.wait_send()
+    for spread in spreads:
+        spread.wait()
 
 
 def finish_kernel(order, merged_ref, cols_ref, new_ref, out_ref):
@@ -183,15 +226,17 @@
             jax.ShapeDtypeStruct((groups, atoms, width), BF16),
         ],
     )(order, *streams, *received, columns, lines)
-    summed = lax.psum_scatter(part.reshape(groups * atoms, width), "src", scatter_dimension=0, tiled=True)
-    updated = pl.pallas_call(
-        atom_kernel,
-        name="atoms",
+    piece = groups * atoms // count_src
+    links = pltpu.SemaphoreType.DMA((count_src - 1,))
+    returned = pl.pallas_call(
+        functools.partial(exchange_kernel, count_src),
+        name="exchange",
         in_specs=[whole] * 4,
         out_specs=whole,
-        out_shape=jax.ShapeDtypeStruct(summed.shape, BF16),
-    )(summed, atom_gain.reshape(1, width), atom_up, atom_down)
-    returned = lax.all_gather(updated, "src", axis=0, tiled=True)
+        out_shape=jax.ShapeDtypeStruct((groups * atoms, width), BF16),
+        scratch_shapes=[pltpu.VMEM((count_src - 1, piece, width), BF16), links, links, links, links],
+        compiler_params=pltpu.CompilerParams(collective_id=0, has_side_effects=True),
+    )(part.reshape(groups * atoms, width), atom_gain.reshape(1, width), atom_up, atom_down)
     out = pl.pallas_call(
         finish_kernel,
         name="finish",

time: 265 us -> 234 us (0.88)
  the two profiles are of different devices: /device:TPU:0 before, /device:TPU:29 now
where the time goes in v2:
time: 234 us
  Pallas kernels  152 us (65%)
  waiting for transfers between devices  69.9 us (30%)
  starting transfers between devices  5.11 us (2%)
  local copies, waits for them, and re-layouts  3.36 us (1%)
  other arithmetic  3.25 us (1%)
    pallas_call x1, Pallas kernels, shards(): pl.pallas_call(functools.partial(exchange_kernel, count_src), name='excha...  103 us
    ppermute x2, waiting for transfers between devices, shards(): received.append(lax.ppermute(start, ('src', 'tgt'), pairs))  69.9 us
    pallas_call x2, Pallas kernels, shards(): pl.pallas_call(stream_kernel, name=f'stream{s}', grid=(rows // wide,), in...  14.6 us
    pallas_call x1, Pallas kernels, shards(): pl.pallas_call(functools.partial(merge_kernel, groups), name='merge', gri...  13.2 us
    pallas_call x2, Pallas kernels, shards(): pl.pallas_call(start_kernel, name=f'start{s}', grid_spec=pltpu.PrefetchSc...  11.2 us
    pallas_call x1, Pallas kernels, shards(): pl.pallas_call(finish_kernel, name='finish', grid_spec=pltpu.PrefetchScal...  9.6 us
    ppermute x2, starting transfers between devices, shards(): received.append(lax.ppermute(start, ('src', 'tgt'), pairs))  5.11 us
  transfers between devices with their start and end apart: 2, of which 2 were waited for; matrix products, arithmetic and copies ran while one was open for 0% of the time, Pallas kernels for 9%

profile of v2, /device:TPU:29, one launch (start us, length us, event | category | flops | bytes accessed | tf_op | source)
XLA Modules:
  0.0 233.5 jit_solution(2303495753968145464)
XLA Ops:
  0.0 0.0 copy-start.2
  0.0 0.7 fusion.2
  0.7 0.4 copy.27
  1.1 1.1 copy.26
  2.2 0.0 copy-done.2
  2.2 0.4 copy.28
  2.5 0.6 pad_add_fusion.1.order
  3.2 1.9 pad_add_fusion.cols_ref.refs_4_
  5.1 5.6 %start0.1.start_ref = bf16[1024,512]{1,0:T(8,128)(2,1)} custom-call(s32[2]{0:T(128)} %pad_add_fusion.1.order, bf16[8,2,128,512]{3,2,1,0:T(8,128)(2,1)} %bitcast.22, s32[2,1024,4]{2,1,0:T(8,128)} %pad_add_fusion.cols_ref.refs_4_, bf16[1024,512]{1,0:T(8,128)(2,1)} %atom_ref.3), custom_call_target="tpu_custom_call" | custom-call | tf_op jit(solution)/shard_map/start0/pallas_call | solution.py:159
  10.7 2.9 %collective-permute-start = (bf16[1024,512]{1,0:T(8,128)(2,1)}, bf16[1024,512]{1,0:T(8,128)(2,1)S(1)}, u32[]{:S(2)}, u32[]{:S(2)}) collective-permute-start(bf16[1024,512]{1,0:T(8,128)(2,1)} %start0.1.start_ref), channel_id=1, source_target_pairs={{0,0},{1,8},{2,16},{3,24},{4,4},{5,12},{6,20},{7,28},{8,1},{9,9},{... | collective-permute-start | bytes 3145736 | tf_op jit(solution)/shard_map/ppermute | solution.py:180
  13.6 5.6 %start1.1.start_ref = bf16[1024,512]{1,0:T(8,128)(2,1)} custom-call(s32[2]{0:T(128)} %pad_add_fusion.1.order, bf16[8,2,128,512]{3,2,1,0:T(8,128)(2,1)} %bitcast.23, s32[2,1024,4]{2,1,0:T(8,128)} %pad_add_fusion.cols_ref.refs_4_, bf16[1024,512]{1,0:T(8,128)(2,1)} %atom_ref.3), custom_call_target="tpu_custom_call" | custom-call | tf_op jit(solution)/shard_map/start1/pallas_call | solution.py:159
  19.1 2.2 collective-permute-start.1
  21.4 0.6 copy.30
  21.9 7.3 %stream0.1.refs_0_ = f32[1024,512]{1,0:T(8,128)} custom-call(bf16[1024,512]{1,0:T(8,128)(2,1)} %start0.1.start_ref, bf16[3,512,512]{2,1,0:T(8,128)(2,1)} %w_in_ref.3, bf16[3,512,512]{2,1,0:T(8,128)(2,1)} %w_out_ref.3, f32[3,512]{1,0:T(4,128)} %gain_ref.3), custom_call_target="tpu_custom_call" | custom-call | flops 3221225472 | bytes 6291456 | tf_op jit(solution)/shard_map/stream0/pallas_call | solution.py:184
  29.2 7.3 %stream1.1.refs_1_ = f32[1024,512]{1,0:T(8,128)} custom-call(bf16[1024,512]{1,0:T(8,128)(2,1)} %start1.1.start_ref, bf16[3,512,512]{2,1,0:T(8,128)(2,1)} %w_in_ref.3, bf16[3,512,512]{2,1,0:T(8,128)(2,1)} %w_out_ref.3, f32[3,512]{1,0:T(4,128)} %gain_ref.3), custom_call_target="tpu_custom_call" | custom-call | flops 3221225472 | bytes 6291456 | tf_op jit(solution)/shard_map/stream1/pallas_call | solution.py:184
  36.5 47.9 %collective-permute-done.refs_2_ = bf16[1024,512]{1,0:T(8,128)(2,1)S(1)} collective-permute-done((bf16[1024,512]{1,0:T(8,128)(2,1)}, bf16[1024,512]{1,0:T(8,128)(2,1)S(1)}, u32[]{:S(2)}, u32[]{:S(2)}) %collective-permute-start) | collective-permute-done | bytes 1048608 | tf_op jit(solution)/shard_map/ppermute | solution.py:180
  84.4 0.0 copy-start
  84.4 22.0 %collective-permute-done.1.refs_3_ = bf16[1024,512]{1,0:T(8,128)(2,1)S(1)} collective-permute-done((bf16[1024,512]{1,0:T(8,128)(2,1)}, bf16[1024,512]{1,0:T(8,128)(2,1)S(1)}, u32[]{:S(2)}, u32[]{:S(2)}) %collective-permute-start.1) | collective-permute-done | bytes 1048608 | tf_op jit(solution)/shard_map/ppermute | solution.py:180
  106.4 0.0 copy-start.1
  106.4 0.0 copy-done
  106.4 1.0 copy-done.1
  107.3 13.2 %merge.1 = (f32[2,1024,512]{2,1,0:T(8,128)}, bf16[2,1024,512]{2,1,0:T(8,128)(2,1)}) custom-call(s32[2]{0:T(128)} %pad_add_fusion.1.order, f32[1024,512]{1,0:T(8,128)} %stream0.1.refs_0_, f32[1024,512]{1,0:T(8,128)} %stream1.1.refs_1_, bf16[1024,512]{1,0:T(8,128)(2,1)} %copy-done, bf16[1024,512]{1,0:T(8,128)(2,1)} %copy-done.1, ...), custom_call_target="tpu_custom_call" | custom-call | tf_op jit(solution)/shard_map/merge/pallas_call | solution.py:203
  120.5 103.4 %exchange.1.new_ref = bf16[2048,512]{1,0:T(8,128)(2,1)} custom-call(bf16[2048,512]{1,0:T(8,128)(2,1)} %bitcast.24, f32[1,512]{1,0:T(1,128)} %bitcast.30, bf16[512,512]{1,0:T(8,128)(2,1)} %up_ref.1, bf16[512,512]{1,0:T(8,128)(2,1)} %down_ref.1), custom_call_target="tpu_custom_call" | custom-call | tf_op jit(solution)/shard_map/exchange/pallas_call | solution.py:231
  223.9 9.6 %finish.1 = bf16[8,2,128,512]{3,2,1,0:T(8,128)(2,1)} custom-call(s32[2]{0:T(128)} %pad_add_fusion.1.order, f32[2,1024,512]{2,1,0:T(8,128)} %get-tuple-element.7.merged_ref, s32[2,1024,4]{2,1,0:T(8,128)} %pad_add_fusion.cols_ref.refs_4_, bf16[2048,512]{1,0:T(8,128)(2,1)} %exchange.1.new_ref), custom_call_target="tpu_custom_call" | custom-call | tf_op jit(solution)/shard_map/finish/pallas_call | solution.py:240
Async XLA Ops:
  0.0 2.2 copy-start.2
  10.7 73.7 %collective-permute-start = (bf16[1024,512]{1,0:T(8,128)(2,1)}, bf16[1024,512]{1,0:T(8,128)(2,1)S(1)}, u32[]{:S(2)}, u32[]{:S(2)}) collective-permute-start(bf16[1024,512]{1,0:T(8,128)(2,1)} %start0.1.start_ref), channel_id=1, source_target_pairs={{0,0},{1,8},{2,16},{3,24},{4,4},{5,12},{6,20},{7,28},{8,1},{9,9},{... | collective-permute-start | bytes 3145736 | tf_op jit(solution)/shard_map/ppermute | solution.py:180
  19.1 87.2 %collective-permute-start.1 = (bf16[1024,512]{1,0:T(8,128)(2,1)}, bf16[1024,512]{1,0:T(8,128)(2,1)S(1)}, u32[]{:S(2)}, u32[]{:S(2)}) collective-permute-start(bf16[1024,512]{1,0:T(8,128)(2,1)} %start1.1.start_ref), channel_id=1, source_target_pairs={{0,4},{1,12},{2,20},{3,28},{4,0},{5,8},{6,16},{7,24},{8,5},{9,13},... | collective-permute-start | bytes 3145736 | tf_op jit(solution)/shard_map/ppermute | solution.py:180
  84.4 22.0 %copy-start = (bf16[1024,512]{1,0:T(8,128)(2,1)}, bf16[1024,512]{1,0:T(8,128)(2,1)S(1)}, u32[]{:S(2)}) copy-start(bf16[1024,512]{1,0:T(8,128)(2,1)S(1)} %collective-permute-done.refs_2_) | copy-start | bytes 3145732
  106.4 1.0 copy-start.1

commit v3 on v1

--- a/solution.py
+++ b/solution.py
@@ -63,10 +63,68 @@
         part_ref[0] = total[...].astype(part_ref.dtype)
 
 
-def atom_kernel(sum_ref, gain_ref, up_ref, down_ref, new_ref):
-    normed = rms_scaled(sum_ref[...].astype(F32), gain_ref[...]).astype(BF16)
+def exchange_kernel(
+    count, part_ref, gain_ref, up_ref, down_ref, new_ref, near, far, paired, near_sems, far_sems, spread_sems, relay_sems
+):
+    me = lax.axis_index("src")
+    piece = part_ref.shape[0] // count
+    lines = count // 2
+    place, side = me // 2, lax.rem(me, 2)
+    partner = me + 1 - 2 * side
+
+    def slot(owner):
+        return pl.ds(pl.multiple_of(owner * piece, piece), piece)
+
+    def send(source, target, sems, index, peer):
+        copy = pltpu.make_async_remote_copy(
+            src_ref=source,
+            dst_ref=target,
+            send_sem=sems.at[0, index],
+            recv_sem=sems.at[1, index],
+            device_id={"src": peer},
+            device_id_type=pl.DeviceIdType.MESH,
+        )
+        copy.start()
+        return copy
+
+    ahead = [lax.rem(place + step, lines) for step in range(1, lines)] + [place]
+    behind = [lax.rem(place - step + lines, lines) for step in range(1, lines)]
+    barrier = pltpu.get_barrier_semaphore()
+    for peer in [partner] + [spot * 2 + side for spot in ahead[:-1]]:
+        pl.semaphore_signal(barrier, inc=1, device_id={"src": peer}, device_id_type=pl.DeviceIdType.MESH)
+    pl.semaphore_wait(barrier, lines)
+
+    shares = [
+        send(part_ref.at[slot(spot * 2 + 1 - side)], near.at[step], near_sems, step, partner)
+        for step, spot in enumerate(ahead)
+    ]
+    sums = []
+    for step, spot in enumerate(ahead):
+        shares[step].wait_recv()
+        total = part_ref[slot(spot * 2 + side)].astype(F32) + near[step].astype(F32)
+        if step < lines - 1:
+            paired[step] = total.astype(BF16)
+            sums.append(send(paired.at[step], far.at[step], far_sems, step, spot * 2 + side))
+    for step in range(lines - 1):
+        sums[step].wait_recv()
+        total = total + far[step].astype(F32)
+    normed = rms_scaled(total, gain_ref[...]).astype(BF16)
     hidden = jax.nn.silu(jnp.dot(normed, up_ref[...], preferred_element_type=F32)).astype(BF16)
-    new_ref[...] = jnp.dot(hidden, down_ref[...], preferred_element_type=F32).astype(BF16)
+    new_ref[slot(me)] = jnp.dot(hidden, down_ref[...], preferred_element_type=F32).astype(BF16)
+
+    own = new_ref.at[slot(me)]
+    spreads = [
+        send(own, own, spread_sems, step, spot * 2 + side) for step, spot in enumerate(ahead[:-1])
+    ]
+    relays = [send(own, own, relay_sems, lines - 1, partner)]
+    for step, spot in enumerate(behind):
+        spreads[step].wait_recv()
+        block = new_ref.at[slot(spot * 2 + side)]
+        relays.append(send(block, block, relay_sems, step, partner))
+    for copy in shares + sums + spreads:
+        copy.wait_send()
+    for copy in relays:
+        copy.wait()
 
 
 def finish_kernel(order, merged_ref, cols_ref, new_ref, out_ref):
@@ -183,15 +241,19 @@
             jax.ShapeDtypeStruct((groups, atoms, width), BF16),
         ],
     )(order, *streams, *received, columns, lines)
-    summed = lax.psum_scatter(part.reshape(groups * atoms, width), "src", scatter_dimension=0, tiled=True)
-    updated = pl.pallas_call(
-        atom_kernel,
-        name="atoms",
+    piece = groups * atoms // count_src
+    lines_src = count_src // 2
+    links = pltpu.SemaphoreType.DMA((2, lines_src))
+    boxes = pltpu.VMEM((lines_src, piece, width), BF16)
+    returned = pl.pallas_call(
+        functools.partial(exchange_kernel, count_src),
+        name="exchange",
         in_specs=[whole] * 4,
         out_specs=whole,
-        out_shape=jax.ShapeDtypeStruct(summed.shape, BF16),
-    )(summed, atom_gain.reshape(1, width), atom_up, atom_down)
-    returned = lax.all_gather(updated, "src", axis=0, tiled=True)
+        out_shape=jax.ShapeDtypeStruct((groups * atoms, width), BF16),
+        scratch_shapes=[boxes, boxes, boxes, links, links, links, links],
+        compiler_params=pltpu.CompilerParams(collective_id=0, has_side_effects=True),
+    )(part.reshape(groups * atoms, width), atom_gain.reshape(1, width), atom_up, atom_down)
     out = pl.pallas_call(
         finish_kernel,
         name="finish",

time: 265 us -> 204 us (0.77)
  the two profiles are of different devices: /device:TPU:0 before, /device:TPU:29 now
where the time goes in v3:
time: 204 us; the launch traced here: 202 us
  Pallas kernels  120 us (59%)
  waiting for transfers between devices  69.9 us (34%)
  starting transfers between devices  5.11 us (3%)
  local copies, waits for them, and re-layouts  3.36 us (2%)
  other arithmetic  3.25 us (2%)
    pallas_call x1, Pallas kernels, shards(): pl.pallas_call(functools.partial(exchange_kernel, count_src), name='excha...  71.5 us
    ppermute x2, waiting for transfers between devices, shards(): received.append(lax.ppermute(start, ('src', 'tgt'), pairs))  69.9 us
    pallas_call x2, Pallas kernels, shards(): pl.pallas_call(stream_kernel, name=f'stream{s}', grid=(rows // wide,), in...  14.6 us
    pallas_call x1, Pallas kernels, shards(): pl.pallas_call(functools.partial(merge_kernel, groups), name='merge', gri...  13.2 us
    pallas_call x2, Pallas kernels, shards(): pl.pallas_call(start_kernel, name=f'start{s}', grid_spec=pltpu.PrefetchSc...  11.2 us
    pallas_call x1, Pallas kernels, shards(): pl.pallas_call(finish_kernel, name='finish', grid_spec=pltpu.PrefetchScal...  9.59 us
    ppermute x2, starting transfers between devices, shards(): received.append(lax.ppermute(start, ('src', 'tgt'), pairs))  5.11 us
  transfers between devices with their start and end apart: 2, of which 2 were waited for; matrix products, arithmetic and copies ran while one was open for 0% of the time, Pallas kernels for 10%

profile of v3, /device:TPU:29, one launch (start us, length us, event | category | flops | bytes accessed | tf_op | source)
XLA Modules:
  0.0 201.6 jit_solution(2379169605636660880)
XLA Ops:
  0.0 0.0 copy-start.2
  0.0 0.7 fusion.2
  0.7 0.4 copy.27
  1.1 1.1 copy.26
  2.2 0.0 copy-done.2
  2.2 0.4 copy.28
  2.5 0.6 pad_add_fusion.1.order
  3.2 1.9 pad_add_fusion.cols_ref.refs_4_
  5.1 5.6 %start0.1.start_ref = bf16[1024,512]{1,0:T(8,128)(2,1)} custom-call(s32[2]{0:T(128)} %pad_add_fusion.1.order, bf16[8,2,128,512]{3,2,1,0:T(8,128)(2,1)} %bitcast.22, s32[2,1024,4]{2,1,0:T(8,128)} %pad_add_fusion.cols_ref.refs_4_, bf16[1024,512]{1,0:T(8,128)(2,1)} %atom_ref.3), custom_call_target="tpu_custom_call" | custom-call | tf_op jit(solution)/shard_map/start0/pallas_call | solution.py:174
  10.7 2.9 %collective-permute-start = (bf16[1024,512]{1,0:T(8,128)(2,1)}, bf16[1024,512]{1,0:T(8,128)(2,1)S(1)}, u32[]{:S(2)}, u32[]{:S(2)}) collective-permute-start(bf16[1024,512]{1,0:T(8,128)(2,1)} %start0.1.start_ref), channel_id=1, source_target_pairs={{0,0},{1,8},{2,16},{3,24},{4,4},{5,12},{6,20},{7,28},{8,1},{9,9},{... | collective-permute-start | bytes 3145736 | tf_op jit(solution)/shard_map/ppermute | solution.py:195
  13.6 5.6 %start1.1.start_ref = bf16[1024,512]{1,0:T(8,128)(2,1)} custom-call(s32[2]{0:T(128)} %pad_add_fusion.1.order, bf16[8,2,128,512]{3,2,1,0:T(8,128)(2,1)} %bitcast.23, s32[2,1024,4]{2,1,0:T(8,128)} %pad_add_fusion.cols_ref.refs_4_, bf16[1024,512]{1,0:T(8,128)(2,1)} %atom_ref.3), custom_call_target="tpu_custom_call" | custom-call | tf_op jit(solution)/shard_map/start1/pallas_call | solution.py:174
  19.1 2.2 %collective-permute-start.1 = (bf16[1024,512]{1,0:T(8,128)(2,1)}, bf16[1024,512]{1,0:T(8,128)(2,1)S(1)}, u32[]{:S(2)}, u32[]{:S(2)}) collective-permute-start(bf16[1024,512]{1,0:T(8,128)(2,1)} %start1.1.start_ref), channel_id=1, source_target_pairs={{0,4},{1,12},{2,20},{3,28},{4,0},{5,8},{6,16},{7,24},{8,5},{9,13},... | collective-permute-start | bytes 3145736 | tf_op jit(solution)/shard_map/ppermute | solution.py:195
  21.4 0.6 copy.30
  21.9 7.3 %stream0.1.refs_0_ = f32[1024,512]{1,0:T(8,128)} custom-call(bf16[1024,512]{1,0:T(8,128)(2,1)} %start0.1.start_ref, bf16[3,512,512]{2,1,0:T(8,128)(2,1)} %w_in_ref.3, bf16[3,512,512]{2,1,0:T(8,128)(2,1)} %w_out_ref.3, f32[3,512]{1,0:T(4,128)} %gain_ref.3), custom_call_target="tpu_custom_call" | custom-call | flops 3221225472 | bytes 6291456 | tf_op jit(solution)/shard_map/stream0/pallas_call | solution.py:199
  29.2 7.3 %stream1.1.refs_1_ = f32[1024,512]{1,0:T(8,128)} custom-call(bf16[1024,512]{1,0:T(8,128)(2,1)} %start1.1.start_ref, bf16[3,512,512]{2,1,0:T(8,128)(2,1)} %w_in_ref.3, bf16[3,512,512]{2,1,0:T(8,128)(2,1)} %w_out_ref.3, f32[3,512]{1,0:T(4,128)} %gain_ref.3), custom_call_target="tpu_custom_call" | custom-call | flops 3221225472 | bytes 6291456 | tf_op jit(solution)/shard_map/stream1/pallas_call | solution.py:199
  36.5 47.9 %collective-permute-done.refs_2_ = bf16[1024,512]{1,0:T(8,128)(2,1)S(1)} collective-permute-done((bf16[1024,512]{1,0:T(8,128)(2,1)}, bf16[1024,512]{1,0:T(8,128)(2,1)S(1)}, u32[]{:S(2)}, u32[]{:S(2)}) %collective-permute-start) | collective-permute-done | bytes 1048608 | tf_op jit(solution)/shard_map/ppermute | solution.py:195
  84.4 0.0 copy-start
  84.4 22.0 %collective-permute-done.1.refs_3_ = bf16[1024,512]{1,0:T(8,128)(2,1)S(1)} collective-permute-done((bf16[1024,512]{1,0:T(8,128)(2,1)}, bf16[1024,512]{1,0:T(8,128)(2,1)S(1)}, u32[]{:S(2)}, u32[]{:S(2)}) %collective-permute-start.1) | collective-permute-done | bytes 1048608 | tf_op jit(solution)/shard_map/ppermute | solution.py:195
  106.4 0.0 copy-start.1
  106.4 0.0 copy-done
  106.4 1.0 copy-done.1
  107.3 13.2 %merge.1 = (f32[2,1024,512]{2,1,0:T(8,128)}, bf16[2,1024,512]{2,1,0:T(8,128)(2,1)}) custom-call(s32[2]{0:T(128)} %pad_add_fusion.1.order, f32[1024,512]{1,0:T(8,128)} %stream0.1.refs_0_, f32[1024,512]{1,0:T(8,128)} %stream1.1.refs_1_, bf16[1024,512]{1,0:T(8,128)(2,1)} %copy-done, bf16[1024,512]{1,0:T(8,128)(2,1)} %copy-done.1, ...), custom_call_target="tpu_custom_call" | custom-call | tf_op jit(solution)/shard_map/merge/pallas_call | solution.py:218
  120.5 71.5 %exchange.1.new_ref = bf16[2048,512]{1,0:T(8,128)(2,1)} custom-call(bf16[2048,512]{1,0:T(8,128)(2,1)} %bitcast.24, f32[1,512]{1,0:T(1,128)} %bitcast.30, bf16[512,512]{1,0:T(8,128)(2,1)} %up_ref.1, bf16[512,512]{1,0:T(8,128)(2,1)} %down_ref.1), custom_call_target="tpu_custom_call" | custom-call | tf_op jit(solution)/shard_map/exchange/pallas_call | solution.py:248
  192.0 9.6 %finish.1 = bf16[8,2,128,512]{3,2,1,0:T(8,128)(2,1)} custom-call(s32[2]{0:T(128)} %pad_add_fusion.1.order, f32[2,1024,512]{2,1,0:T(8,128)} %get-tuple-element.7.merged_ref, s32[2,1024,4]{2,1,0:T(8,128)} %pad_add_fusion.cols_ref.refs_4_, bf16[2048,512]{1,0:T(8,128)(2,1)} %exchange.1.new_ref), custom_call_target="tpu_custom_call" | custom-call | tf_op jit(solution)/shard_map/finish/pallas_call | solution.py:257
Async XLA Ops:
  0.0 2.2 %copy-start.2 = (s32[2048]{0:T(1024)S(1)}, s32[2048]{0:T(1024)}, u32[]{:S(2)}) copy-start(s32[2048]{0:T(1024)} %param.14) | copy-start | bytes 24580
  10.7 73.7 %collective-permute-start = (bf16[1024,512]{1,0:T(8,128)(2,1)}, bf16[1024,512]{1,0:T(8,128)(2,1)S(1)}, u32[]{:S(2)}, u32[]{:S(2)}) collective-permute-start(bf16[1024,512]{1,0:T(8,128)(2,1)} %start0.1.start_ref), channel_id=1, source_target_pairs={{0,0},{1,8},{2,16},{3,24},{4,4},{5,12},{6,20},{7,28},{8,1},{9,9},{... | collective-permute-start | bytes 3145736 | tf_op jit(solution)/shard_map/ppermute | solution.py:195
  19.1 87.2 %collective-permute-start.1 = (bf16[1024,512]{1,0:T(8,128)(2,1)}, bf16[1024,512]{1,0:T(8,128)(2,1)S(1)}, u32[]{:S(2)}, u32[]{:S(2)}) collective-permute-start(bf16[1024,512]{1,0:T(8,128)(2,1)} %start1.1.start_ref), channel_id=1, source_target_pairs={{0,4},{1,12},{2,20},{3,28},{4,0},{5,8},{6,16},{7,24},{8,5},{9,13},... | collective-permute-start | bytes 3145736 | tf_op jit(solution)/shard_map/ppermute | solution.py:195
  84.4 22.0 %copy-start = (bf16[1024,512]{1,0:T(8,128)(2,1)}, bf16[1024,512]{1,0:T(8,128)(2,1)S(1)}, u32[]{:S(2)}) copy-start(bf16[1024,512]{1,0:T(8,128)(2,1)S(1)} %collective-permute-done.refs_2_) | copy-start | bytes 3145732
  106.4 1.0 copy-start.1
